TPU v7x, 32 devices: a whole 2x2x4 slice. The times are simulated.
32 devices in a mesh: section: 2 (over core), fsdp: 4 (over z), dp: 4 (over y, x).
Axes of the slice: x: 2, y: 2, z: 4, core: 2. Of those that a mesh axis runs over, the one named last changes fastest.
Arguments:
- tokens: bfloat16 [1, 16, 128, 1024], P(None, ('fsdp', 'dp')), may hold values from -6 to 6
- segments: int32 [1, 16, 128], P(None, ('fsdp', 'dp')), may hold values from 0 to 3, never falling along the last dimension, each value on 1 to 64 neighbouring positions
- cotangent: float32 [1, 16, 128, 1024], P(None, ('fsdp', 'dp')), may hold values from -6 to 6
- norm_gains: bfloat16 [2, 2, 1024], P('section', None, 'fsdp'), may hold values from 0.5 to 1.5
- proj_weight: bfloat16 [2, 1024, 3072], P('section', 'fsdp'), may hold values from -0.1875 to 0.1875
- rate_weight: bfloat16 [2, 1024, 8], P('section', 'fsdp'), may hold values from -0.1875 to 0.1875
- out_weight: bfloat16 [2, 1024, 1024], P('section', 'fsdp'), may hold values from -0.375 to 0.375
- up_weight: bfloat16 [2, 1024, 5632], P('section', 'fsdp'), may hold values from -0.1875 to 0.1875
- down_weight: bfloat16 [2, 1024, 2816], P('section', 'fsdp'), may hold values from -0.21875 to 0.21875
- conv_kernels: float32 [2, 4, 2048], P('section'), may hold values from -3 to 3
- head_params: float32 [2, 2, 4], P('section'), may hold values from -2.5 to 0.5
- out_gain: float32 [2, 256], P('section'), may hold values from 0.5 to 1.5
Outputs:
- section_output: bfloat16 [2, 1, 16, 128, 1024], P('section', None, ('fsdp', 'dp'))
- input_grad: float32 [2, 1, 16, 128, 1024], P('section', None, ('fsdp', 'dp'))
- gains_grad: float32 [2, 2, 1024], P('section', None, 'fsdp')
- proj_grad: float32 [2, 1024, 3072], P('section', 'fsdp')
- rate_grad: float32 [2, 1024, 8], P('section', 'fsdp')
- out_grad: float32 [2, 1024, 1024], P('section', 'fsdp')
- up_grad: float32 [2, 1024, 5632], P('section', 'fsdp')
- down_grad: float32 [2, 1024, 2816], P('section', 'fsdp')
- kernel_grad: float32 [2, 4, 2048], P('section')
- head_grad: float32 [2, 2, 4], P('section')
- out_gain_grad: float32 [2, 256], P('section')
Inputs may be any that keep to these rules, and one draw needn't show every extreme that they name: `segments`: within each sequence the numbers never fall, every one of 0 .. 3 occurs, and each document holds 1 to 64 positions, one exactly 64.
All inputs are finite; a program needn't handle non-finite values.
Results may differ from a plain program's by a relative error of at most 0.034.
Values may be sent and summed in bfloat16 or wider, within the bound.
A program may use at most 256 MiB of HBM per device.

v0:
```python
from functools import partial
import jax
import jax.numpy as jnp
from jax import lax
from jax.sharding import PartitionSpec as P

SPAN = 64
highest = lax.Precision.HIGHEST
reset_level = -30.0


def passed_along(value, axis, steps):
    count = lax.axis_size(axis)
    leading, last = (max(0, -steps), min(count, count - steps))
    return lax.ppermute(value, axis, [(source, source + steps) for source in range(leading, last)])


def rms_gain(values, gain_vec):
    return values * lax.rsqrt(jnp.mean(values * values, -1, keepdims=True) + 1e-06) * gain_vec


def swiglu(joined):
    half_width = joined.shape[-1] // 2
    return jax.nn.silu(joined[..., :half_width]) * joined[..., half_width:]


def short_conv(raw_input, kernel, segment):
    length = raw_input.shape[1]
    tap_count = kernel.shape[0]
    total = raw_input * kernel[tap_count - 1]
    for offset in range(1, tap_count):
        shifted = jnp.pad(raw_input, ((0, 0), (offset, 0), (0, 0)))[:, :length]
        earlier = jnp.pad(segment, ((0, 0), (offset, 0)), constant_values=-1)[:, :length]
        total = (
            total
            + jnp.where((earlier == segment)[..., None], shifted, 0.0)
            * kernel[tap_count - 1 - offset]
        )
    return jax.nn.silu(total)


def delta_rule(queries, key_rows, value_rows, beta_gate, decays, block_len):
    batch_size, head_count, length, key_dim = queries.shape
    value_dim = value_rows.shape[-1]
    block_count = length // block_len

    def to_blocks(array):
        return array.reshape(array.shape[:2] + (block_count, block_len) + array.shape[3:])

    queries = to_blocks(queries)
    key_rows = to_blocks(key_rows)
    value_rows = to_blocks(value_rows)
    beta_gate = to_blocks(beta_gate)
    levels = jnp.cumsum(to_blocks(decays), axis=-1)
    places = jnp.arange(block_len)
    lower_mask = places[:, None] >= places[None, :]
    strict_mask = places[:, None] > places[None, :]
    spread = jnp.exp(jnp.where(lower_mask, levels[..., :, None] - levels[..., None, :], -1e30))
    beta_keys = key_rows * beta_gate[..., None]
    key_inner = jnp.einsum("bhncd,bhnmd->bhncm", beta_keys, key_rows, precision=highest) * spread
    system = jnp.where(strict_mask, key_inner, 0.0)
    right_side = jnp.concatenate(
        [beta_keys * jnp.exp(levels)[..., None], value_rows * beta_gate[..., None]], -1
    )
    solved = lax.linalg.triangular_solve(
        system, right_side, left_side=True, lower=True, unit_diagonal=True
    )
    solved_keys = solved[..., :key_dim]
    solved_values = solved[..., key_dim:]
    scores = jnp.einsum("bhncd,bhnmd->bhncm", queries, key_rows, precision=highest) * spread
    fading = queries * jnp.exp(levels)[..., None]
    final_level = levels[..., -1:]
    carried = key_rows * jnp.exp(final_level - levels)[..., None]

    def advance(memory, pieces):
        fading_part, keys_part, values_part, scores_part, carried_part, final_part = pieces
        update = values_part - jnp.einsum("bhcd,bhde->bhce", keys_part, memory, precision=highest)
        output = jnp.einsum("bhcd,bhde->bhce", fading_part, memory, precision=highest) + jnp.einsum(
            "bhcm,bhme->bhce", scores_part, update, precision=highest
        )
        memory = memory * jnp.exp(final_part)[..., None] + jnp.einsum(
            "bhcd,bhce->bhde", carried_part, update, precision=highest
        )
        return (memory, output)

    pieces = tuple(
        (
            jnp.moveaxis(array, 2, 0)
            for array in (fading, solved_keys, solved_values, scores, carried, final_level)
        )
    )
    initial = jnp.zeros((batch_size, head_count, key_dim, value_dim), queries.dtype)
    _, outputs = lax.scan(advance, initial, pieces)
    return jnp.moveaxis(outputs, 0, 2).reshape(batch_size, head_count, length, value_dim)


def token_mixer(projected, rate_logits, kernel, head_params, out_gain, segment):
    batch_size, length, _ = projected.shape
    head_count = head_params.shape[1]
    value_dim = out_gain.shape[0]
    channels = kernel.shape[1]
    key_width = (channels - head_count * value_dim) // 2
    key_dim = key_width // head_count
    mixed = short_conv(projected[..., :channels], kernel, segment)

    def heads_of(array, size):
        return jnp.moveaxis(array.reshape(batch_size, length, head_count, size), 2, 1)

    queries = heads_of(mixed[..., :key_width], key_dim)
    key_rows = heads_of(mixed[..., key_width : 2 * key_width], key_dim)
    value_rows = heads_of(mixed[..., 2 * key_width :], value_dim)
    queries = (
        queries
        * lax.rsqrt(jnp.sum(queries * queries, -1, keepdims=True) + 1e-06)
        * key_dim ** (-0.5)
    )
    key_rows = key_rows * lax.rsqrt(jnp.sum(key_rows * key_rows, -1, keepdims=True) + 1e-06)
    beta_gate = jax.nn.sigmoid(jnp.moveaxis(rate_logits[..., head_count:], 2, 1))
    decays = -jnp.exp(head_params[0])[:, None] * jax.nn.softplus(
        jnp.moveaxis(rate_logits[..., :head_count], 2, 1) + head_params[1][:, None]
    )
    earlier = jnp.pad(segment, ((0, 0), (1, 0)), constant_values=-1)[:, :length]
    decays = jnp.where((earlier != segment)[:, None, :], reset_level, decays)
    output = delta_rule(queries, key_rows, value_rows, beta_gate, decays, SPAN)
    output = output * lax.rsqrt(jnp.mean(output * output, -1, keepdims=True) + 1e-05) * out_gain
    gating = heads_of(projected[..., channels:], value_dim)
    return jnp.moveaxis(output * jax.nn.silu(gating), 1, 2).reshape(
        batch_size, length, head_count * value_dim
    )


def last_contract(left, right):
    return lax.dot_general(
        left, right, (((2,), (1,)), ((), ())), preferred_element_type=jnp.float32
    )


def layer_forward(entering, segment, weights, small_params):
    norm_gains, proj_weight, rate_weight, out_weight, up_weight, down_weight = weights
    kernel, head_params, out_gain = small_params
    widened = entering.astype(jnp.float32)
    normed_one, norm_one_back = jax.vjp(rms_gain, widened, norm_gains[0].astype(jnp.float32))
    hidden_one = normed_one.astype(jnp.bfloat16)
    projected = jnp.dot(hidden_one, proj_weight, preferred_element_type=jnp.float32)
    rate_logits = jnp.dot(hidden_one, rate_weight, preferred_element_type=jnp.float32)
    mixed_out, mixer_back = jax.vjp(
        partial(token_mixer, segment=segment), projected, rate_logits, kernel, head_params, out_gain
    )
    mixed_half = mixed_out.astype(jnp.bfloat16)
    stream = widened + last_contract(mixed_half, out_weight)
    normed_two, norm_two_back = jax.vjp(rms_gain, stream, norm_gains[1].astype(jnp.float32))
    hidden_two = normed_two.astype(jnp.bfloat16)
    gate_up = jnp.dot(hidden_two, up_weight, preferred_element_type=jnp.float32)
    activated, act_back = jax.vjp(swiglu, gate_up)
    act_half = activated.astype(jnp.bfloat16)
    layer_out = (stream + last_contract(act_half, down_weight)).astype(jnp.bfloat16)
    residuals = (
        norm_one_back,
        hidden_one,
        mixer_back,
        mixed_half,
        norm_two_back,
        hidden_two,
        act_back,
        act_half,
    )
    return (layer_out, residuals)


def layer_backward(cotangent_in, residuals, weights):
    norm_gains, proj_weight, rate_weight, out_weight, up_weight, down_weight = weights
    (
        norm_one_back,
        hidden_one,
        mixer_back,
        mixed_half,
        norm_two_back,
        hidden_two,
        act_back,
        act_half,
    ) = residuals
    dout_half = cotangent_in.astype(jnp.bfloat16)
    (gate_up_grad,) = act_back(jnp.dot(dout_half, down_weight, preferred_element_type=jnp.float32))
    gate_up_cot = gate_up_grad.astype(jnp.bfloat16)
    stream_grad, gain_two = norm_two_back(last_contract(gate_up_cot, up_weight))
    stream_grad = cotangent_in + stream_grad
    branch_cot = stream_grad.astype(jnp.bfloat16)
    proj_grad, rate_grad, kernel_grad, head_grad, out_gain_grad = mixer_back(
        jnp.dot(branch_cot, out_weight, preferred_element_type=jnp.float32)
    )
    proj_cot = proj_grad.astype(jnp.bfloat16)
    rate_cot = rate_grad.astype(jnp.bfloat16)
    hidden_grad = last_contract(proj_cot, proj_weight) + last_contract(rate_cot, rate_weight)
    entry_grad, gain_one = norm_one_back(hidden_grad)
    pairs = (
        hidden_one,
        proj_cot,
        rate_cot,
        mixed_half,
        branch_cot,
        hidden_two,
        gate_up_cot,
        act_half,
        dout_half,
    )
    return (
        stream_grad + entry_grad,
        pairs,
        (kernel_grad, head_grad, out_gain_grad),
        jnp.stack([gain_one, gain_two]),
    )


def weight_terms(pairs, gain_sum, start, count):
    flattened = [member.reshape(-1, member.shape[-1]) for member in pairs]
    (
        hidden_one,
        proj_cot,
        rate_cot,
        mixed_half,
        branch_cot,
        hidden_two,
        gate_up_cot,
        act_half,
        dout_half,
    ) = flattened

    def product(left, right):
        return lax.dot_general(
            left, right, (((0,), (0,)), ((), ())), preferred_element_type=jnp.float32
        )

    return jnp.concatenate(
        [
            product(hidden_one, proj_cot),
            product(hidden_one, rate_cot),
            product(branch_cot, mixed_half),
            product(hidden_two, gate_up_cot),
            product(dout_half, act_half),
            gain_sum.T,
        ],
        1,
    )


def split_term(total, widths):
    pieces = []
    column = 0
    for width in widths:
        pieces.append(total[..., column : column + width])
        column = column + width
    return pieces


def pass_forward(layer_out):
    return passed_along(layer_out, "section", 1)


def pass_backward(entry_grad):
    return passed_along(entry_grad.astype(jnp.bfloat16), "section", -1).astype(entry_grad.dtype)


def shards(
    tokens,
    segments,
    cotangent,
    norm_gains,
    proj_weight,
    rate_weight,
    out_weight,
    up_weight,
    down_weight,
    conv_kernels,
    head_params,
    out_gain,
):
    first_section = lax.axis_index("section") == 0
    weights = (
        lax.all_gather(norm_gains[0], "fsdp", axis=1, tiled=True),
        lax.all_gather(proj_weight[0], "fsdp", axis=0, tiled=True),
        lax.all_gather(rate_weight[0], "fsdp", axis=0, tiled=True),
        lax.all_gather(out_weight[0], "fsdp", axis=0, tiled=True),
        lax.all_gather(up_weight[0], "fsdp", axis=0, tiled=True),
        lax.all_gather(down_weight[0], "fsdp", axis=0, tiled=True),
    )
    small_params = (conv_kernels[0], head_params[0], out_gain[0])
    batches = tokens.shape[0]
    records = []
    results = []
    for forward_step in range(batches + 1):
        ahead_batch = min(forward_step, batches - 1)
        behind = max(forward_step - 1, 0)
        segment = jnp.where(first_section, segments[ahead_batch], segments[behind])
        if forward_step == 0:
            entering = tokens[0]
        else:
            entering = jnp.where(first_section, tokens[ahead_batch], pass_forward(results[-1]))
        produced, residuals = layer_forward(entering, segment, weights, small_params)
        records.append(residuals)
        results.append(produced)
    incoming = []
    kept_pairs = []
    small_list = []
    gain_list = []
    for backward_step in range(batches + 1):
        if backward_step < batches:
            own_cot = cotangent[batches - 1 - backward_step]
        else:
            own_cot = jnp.zeros_like(cotangent[0])
        if backward_step == 0:
            upstream = jnp.zeros_like(own_cot)
        else:
            upstream = pass_backward(incoming[-1])
        dout_full = jnp.where(first_section, upstream, own_cot)
        entry_grad, pairs, small_grads, gains_step = layer_backward(
            dout_full, records[batches - backward_step], weights
        )
        incoming.append(entry_grad)
        kept_pairs.append(pairs)
        small_list.append(small_grads)
        gain_list.append(gains_step)
    pairs_all = tuple((jnp.concatenate([member[i] for member in kept_pairs], 1) for i in range(9)))
    gain_sum = sum(gain_list)
    small_sum = tuple((sum((member[i] for member in small_list)) for i in range(3)))
    section_output = jnp.stack([jnp.where(first_section, results[0], results[1])])[None]
    input_grad = jnp.stack([jnp.where(first_section, incoming[batches], incoming[batches - 1])])[
        None
    ]
    own_rows = proj_weight.shape[1]
    term_of = partial(weight_terms, pairs_all, gain_sum)
    totals = lax.psum_scatter(
        term_of(jnp.int32(0), own_rows * lax.axis_size("fsdp")).astype(jnp.bfloat16),
        "fsdp",
        scatter_dimension=0,
        tiled=True,
    ).astype(jnp.float32)
    totals = lax.psum(totals.astype(jnp.bfloat16), "dp").astype(jnp.float32)
    kernel_grad, head_grad, out_gain_grad = lax.psum(
        (small_sum[0], small_sum[1], small_sum[2]), ("fsdp", "dp")
    )
    widths = [
        proj_weight.shape[2],
        rate_weight.shape[2],
        out_weight.shape[2],
        up_weight.shape[2],
        down_weight.shape[2],
        2,
    ]
    pieces = split_term(totals, widths)
    return (
        section_output,
        input_grad,
        pieces[5].T[None],
        pieces[0][None],
        pieces[1][None],
        pieces[2][None],
        pieces[3][None],
        pieces[4][None],
        kernel_grad[None],
        head_grad[None],
        out_gain_grad[None],
    )


def solution(mesh):
    return jax.shard_map(
        shards,
        mesh=mesh,
        in_specs=(
            P(None, ("fsdp", "dp"), None, None),
            P(None, ("fsdp", "dp"), None),
            P(None, ("fsdp", "dp"), None, None),
            P("section", None, "fsdp"),
            P("section", "fsdp", None),
            P("section", "fsdp", None),
            P("section", "fsdp", None),
            P("section", "fsdp", None),
            P("section", "fsdp", None),
            P("section", None, None),
            P("section", None, None),
            P("section", None),
        ),
        out_specs=(
            P("section", None, ("fsdp", "dp"), None, None),
            P("section", None, ("fsdp", "dp"), None, None),
            P("section", None, "fsdp"),
            P("section", "fsdp", None),
            P("section", "fsdp", None),
            P("section", "fsdp", None),
            P("section", "fsdp", None),
            P("section", "fsdp", None),
            P("section", None, None),
            P("section", None, None),
            P("section", None),
        ),
        check_vma=False,
    )
```

profile of v0, /device:TPU:0, one launch (start us, length us, event | category | flops | bytes accessed | tf_op | source)
XLA Modules:
  0.0 1455.5 jit_solution(11192671535240137623)
XLA Ops:
  10.3 12.7 all-gather
  23.2 13.7 all-gather.1
  41.3 86.5 %all-gather.11.cloned.1.call-done = bf16[1,1024,3072]{2,1,0:T(8,128)(2,1)} async-done(((bf16[1,256,3072]{2,1,0:T(8,128)(2,1)}), bf16[1,1024,3072]{2,1,0:T(8,128)(2,1)}) %all-gather.11.cloned.1.call-update) | async-done | bytes 6291472 | tf_op jit(solution)/shard_map/all_gather | solution.py:280
  141.4 39.3 %custom-call.16 = f32[1,4,2,1,64,64]{4,5,3,2,1,0:T(8,128)S(1)} custom-call(f32[1,4,2,1,64,64]{5,4,3,2,1,0:T(8,128)S(1)} %fusion.409), custom_call_target="InvertDiagBlocksLowerTriangular" | custom-call | tf_op jit(solution)/shard_map/jvp()/triangular_solve/custom-call.1 | solution.py:65
  185.2 7.1 while.96
  201.8 173.0 %all-gather.15.cloned.1.call-done = bf16[1,1024,5632]{2,1,0:T(8,128)(2,1)} async-done(((bf16[1,256,5632]{2,1,0:T(8,128)(2,1)}), bf16[1,1024,5632]{2,1,0:T(8,128)(2,1)}) %all-gather.15.cloned.1.call-update) | async-done | bytes 11534352 | tf_op jit(solution)/shard_map/all_gather | solution.py:283
  374.8 6.0 fusion.166
  382.8 98.3 %all-gather.17.cloned.1.call-done = bf16[1,1024,2816]{2,1,0:T(8,128)(2,1)} async-done(((bf16[1,256,2816]{2,1,0:T(8,128)(2,1)}), bf16[1,1024,2816]{2,1,0:T(8,128)(2,1)}) %all-gather.17.cloned.1.call-update) | async-done | bytes 5767184 | tf_op jit(solution)/shard_map/all_gather | solution.py:284
  481.2 4.6 fusion.242
  515.8 40.7 %custom-call.17 = f32[1,4,2,1,64,64]{4,5,3,2,1,0:T(8,128)} custom-call(f32[1,4,2,1,64,64]{5,4,3,2,1,0:T(8,128)} %fusion.397), custom_call_target="InvertDiagBlocksLowerTriangular" | custom-call | tf_op jit(solution)/shard_map/jvp()/triangular_solve/custom-call.1 | solution.py:65
  576.0 11.5 while.97
  599.8 6.1 fusion.169
  622.0 26.4 %while.98 = (s32[]{:T(128)}, f32[1,4,128,256]{2,3,1,0:T(8,128)S(1)}, f32[2,1,4,64,128]{4,3,0,2,1:T(8,128)}, f32[2,1,4,64,128]{4,3,2,1,0:T(8,128)}, f32[2,1,4,64,...) while((s32[]{:T(128)}, ...), condition=%wide.region_20.23_spmd.clone, body=%wide.region_18.22_spmd.clone.sunk | while | flops 706019328 | bytes 25702096 | solution.py:93
  702.5 4.9 fusion.436
  720.8 19.1 %while.99 = (s32[]{:T(128)}, f32[1,4,128,256]{2,3,1,0:T(8,128)S(1)}, f32[2,1,4,64,128]{4,3,0,2,1:T(8,128)}, f32[2,1,4,64,128]{4,3,2,1,0:T(8,128)}, f32[2,1,4,64,...) while((s32[]{:T(128)}, ...), condition=%wide.region_37.42_spmd.clone, body=%wide.region_35.41_spmd.clone.sunk | while | flops 706019328 | bytes 25701472 | solution.py:93
  762.4 5.6 multiply_reduce_fusion.3
  785.2 4.5 convolution_convert_fusion.2
  796.2 7.3 convolution_convert_fusion
  803.8 5.7 convolution_convert_fusion.1
  809.5 48.0 %concatenate.48 = bf16[1024,12554]{1,0:T(8,128)(2,1)} concatenate(bf16[1024,3072]{1,0:T(8,128)(2,1)} %convolution_convert_fusion.2, bf16[1024,8]{1,0:T(8,128)(2,1)S(1)} %copy.593, bf16[1024,1024]{1,0:T(8,128)(2,1)S(1)} %copy-done.42, bf16[1024,5632]{1,0:T(8,128)(2,1)} %convolution_convert_fusion, bf16[1024,2816]{1,0:T(8,128)(2,1)} %convolution_convert_fusion.1, ...), dimensions={1} | concatenate | bytes 51421184 | tf_op jit(solution)/shard_map/concatenate | solution.py:233
  857.5 427.1 %reduce-scatter.2.cloned.1.call-done = bf16[256,12554]{1,0:T(8,128)(2,1)} async-done(((bf16[1024,12554]{1,0:T(8,128)(2,1)}), bf16[256,12554]{1,0:T(8,128)(2,1)}) %reduce-scatter.2.cloned.1.call-update) | async-done | bytes 6427664 | tf_op jit(solution)/shard_map/reduce_scatter | solution.py:331
  1285.9 5.3 fusion.264
  1291.4 79.9 %all-reduce.51 = (f32[1,4,2048]{2,1,0:T(4,128)}, f32[1,2,4]{2,1,0:T(2,128)}, f32[1,256]{1,0:T(1,128)}) all-reduce(f32[1,4,2048]{2,1,0:T(4,128)S(1)} %add_bitcast_fusion.2, f32[1,2,4]{2,1,0:T(2,128)S(1)} %add_bitcast_fusion.3, f32[1,256]{1,0:T(1,128)S(1)} %bitcast.1621), channel_id=1, replica_groups=mesh['section'=2,'fsdp'=4,'dp'=4] {'fsdp','dp'}, use_global_device_ids=true, to_apply=%region_64.69 | all-reduce | flops 8456 | bytes 67648 | tf_op jit(solution)/shard_map/psum | solution.py:338
  1371.3 62.2 %all-reduce.54.cloned.1.call-done = bf16[256,12554]{1,0:T(8,128)(2,1)} async-done(((bf16[256,12554]{1,0:T(8,128)(2,1)}), bf16[256,12554]{1,0:T(8,128)(2,1)}) %all-reduce.54.cloned.1.call-update) | async-done | bytes 6427664 | tf_op jit(solution)/shard_map/psum | solution.py:337
  (1054 shorter events, 303.8 us)
Async XLA Ops:
  7.2 120.7 %all-gather.11.cloned.1.call-start = ((), (), s32[]{:S(2)}) async-start(), calls=%async_computation.3 | async-start | bytes 7864320 | tf_op jit(solution)/shard_map/all_gather | solution.py:280
  7.9 191.2 %all-gather.13.cloned.1.call-start = ((), (), s32[]{:S(2)}) async-start(), calls=%async_computation.4 | async-start | bytes 2621440 | tf_op jit(solution)/shard_map/all_gather | solution.py:282
  8.7 366.1 %all-gather.15.cloned.1.call-start = ((), (), s32[]{:S(2)}) async-start(), calls=%async_computation.5 | async-start | bytes 14417920 | tf_op jit(solution)/shard_map/all_gather | solution.py:283
  9.5 471.7 %all-gather.17.cloned.1.call-start = ((), (), s32[]{:S(2)}) async-start(), calls=%async_computation.6 | async-start | bytes 7208960 | tf_op jit(solution)/shard_map/all_gather | solution.py:284
  10.0 1274.6 %reduce-scatter.2.cloned.1.call-start = ((), (), s32[]{:S(2)}) async-start(), calls=%async_computation.1 | async-start | bytes 32440320 | tf_op jit(solution)/shard_map/reduce_scatter | solution.py:331
  10.1 130.4 %copy-start.154 = (f32[64,64]{1,0:T(8,128)}, f32[64,64]{1,0:T(8,128)S(1)}, u32[]{:S(2)}) copy-start(f32[64,64]{1,0:T(8,128)S(1)} %get-tuple-element.1668) | copy-start | bytes 49156
  10.1 130.4 %copy-start.161 = (pred[64,64]{1,0:T(8,128)(4,1)}, pred[64,64]{1,0:T(8,128)(4,1)S(1)}, u32[]{:S(2)}) copy-start(pred[64,64]{1,0:T(8,128)(4,1)S(1)} %get-tuple-element.1667) | copy-start | bytes 12292
  10.3 121.5 %copy-start.198 = (pred[128]{0:T(512)(128)(4,1)}, pred[128]{0:T(512)(128)(4,1)S(1)}, u32[]{:S(2)}) copy-start(pred[128]{0:T(512)(128)(4,1)S(1)} %get-tuple-element.1642) | copy-start | bytes 388
  10.3 121.5 %copy-start.202 = (pred[128]{0:T(512)(128)(4,1)}, pred[128]{0:T(512)(128)(4,1)S(1)}, u32[]{:S(2)}) copy-start(pred[128]{0:T(512)(128)(4,1)S(1)} %get-tuple-element.1646) | copy-start | bytes 388
  10.3 121.5 %copy-start.206 = (pred[128]{0:T(512)(128)(4,1)}, pred[128]{0:T(512)(128)(4,1)S(1)}, u32[]{:S(2)}) copy-start(pred[128]{0:T(512)(128)(4,1)S(1)} %get-tuple-element.1647) | copy-start | bytes 388
  23.0 351.8 %copy-start.151 = (f32[1,1,1024]{2,1,0:T(1,128)}, f32[1,1,1024]{2,1,0:T(1,128)S(1)}, u32[]{:S(2)}) copy-start(f32[1,1,1024]{2,1,0:T(1,128)S(1)} %get-tuple-element.1629) | copy-start | bytes 12292
  23.0 468.9 %copy-start.149 = (f32[1,1,1024]{2,1,0:T(1,128)}, f32[1,1,1024]{2,1,0:T(1,128)S(1)}, u32[]{:S(2)}) copy-start(f32[1,1,1024]{2,1,0:T(1,128)S(1)} %get-tuple-element.1630) | copy-start | bytes 12292
  23.2 108.5 %copy-start.239 = (f32[128]{0:T(128)}, f32[128]{0:T(128)S(1)}, u32[]{:S(2)}) copy-start(f32[128]{0:T(128)S(1)} %fusion.515) | copy-start | bytes 1540
  36.9 455.1 %copy-start.159 = (bf16[1,1024,8]{1,2,0:T(8,128)(2,1)}, bf16[1,1024,8]{1,2,0:T(8,128)(2,1)S(1)}, u32[]{:S(2)}) copy-start(bf16[1,1024,8]{1,2,0:T(8,128)(2,1)S(1)} %all-gather.1) | copy-start | bytes 49156
  40.5 97.1 %copy-start.177 = (f32[4,2,64]{2,1,0:T(2,128)}, f32[4,2,64]{2,1,0:T(2,128)S(1)}, u32[]{:S(2)}) copy-start(f32[4,2,64]{2,1,0:T(2,128)S(1)} %get-tuple-element.1632) | copy-start | bytes 6148
  40.5 97.1 %copy-start.181 = (f32[4,2,64]{2,1,0:T(2,128)}, f32[4,2,64]{2,1,0:T(2,128)S(1)}, u32[]{:S(2)}) copy-start(f32[4,2,64]{2,1,0:T(2,128)S(1)} %get-tuple-element.1633) | copy-start | bytes 6148
  40.6 140.2 %copy-start.155 = (f32[4,2,64]{2,1,0:T(2,128)}, f32[4,2,64]{2,1,0:T(2,128)S(1)}, u32[]{:S(2)}) copy-start(f32[4,2,64]{2,1,0:T(2,128)S(1)} %mul.1564) | copy-start | bytes 6148
  201.8 179.1 %copy-start.275 = (f32[128]{0:T(128)}, f32[128]{0:T(128)S(1)}, u32[]{:S(2)}) copy-start(f32[128]{0:T(128)S(1)} %get-tuple-element.1648) | copy-start | bytes 1540
  201.8 279.4 %copy-start.2 = (f32[128,1024]{1,0:T(8,128)}, f32[128,1024]{1,0:T(8,128)S(1)}, u32[]{:S(2)}) copy-start(f32[128,1024]{1,0:T(8,128)S(1)} %get-tuple-element.1649) | copy-start | bytes 1572868
  201.8 179.0 %copy-start.241 = (f32[128]{0:T(128)}, f32[128]{0:T(128)S(1)}, u32[]{:S(2)}) copy-start(f32[128]{0:T(128)S(1)} %fusion.516) | copy-start | bytes 1540
  382.8 103.0 %copy-start.68 = (bf16[1,128,2816]{2,1,0:T(8,128)(2,1)}, bf16[1,128,2816]{2,1,0:T(8,128)(2,1)S(1)}, u32[]{:S(2)}) copy-start(bf16[1,128,2816]{2,1,0:T(8,128)(2,1)S(1)} %multiply_convert_fusion.1) | copy-start | bytes 2162692
  485.8 5.9 collective-permute-start
  697.8 4.6 collective-permute-start.1
  857.5 576.0 %all-reduce.54.cloned.1.call-start = ((), (), s32[]{:S(2)}) async-start(), calls=%async_computation.2 | async-start | bytes 12976128 | tf_op jit(solution)/shard_map/psum | solution.py:337
  (320 other events, 1955.4 us)
Sparse Core Ops, SparseCore 0:
  9.6 118.2 all-gather.10
  129.4 44.0 all-gather.12
  175.1 199.6 all-gather.14
  376.2 104.9 all-gather.16
  857.6 426.9 reduce-scatter.1
  1287.8 145.6 all-reduce.53
where the time goes:
time: 1470 us; the launch traced here: 1460 us
  waiting for transfers between devices  850 us (58%)
  other arithmetic  163 us (11%)
  local copies, waits for them, and re-layouts  161 us (11%)
  matrix products  151 us (10%)
  blocking collectives  106 us (7%)
  between operations  17.9 us (1%)
    reduce_scatter x1, waiting for transfers between devices, shards(): lax.psum_scatter(term_of(jnp.int32(0), own_rows * lax.axis_size('fsdp'))....  427 us
    all_gather x1, waiting for transfers between devices, shards(): lax.all_gather(up_weight[0], 'fsdp', axis=0, tiled=True)  173 us
    all_gather x1, waiting for transfers between devices, shards(): lax.all_gather(down_weight[0], 'fsdp', axis=0, tiled=True)  98.3 us
    all_gather x1, waiting for transfers between devices, shards(): lax.all_gather(proj_weight[0], 'fsdp', axis=0, tiled=True)  86.5 us
    another operation x6, other arithmetic, delta_rule(): lax.linalg.triangular_solve(system, right_side, left_side=True, lower=Tru...  83.3 us
    psum x1, blocking collectives, shards(): lax.psum((small_sum[0], small_sum[1], small_sum[2]), ('fsdp', 'dp'))  79.9 us
    psum x1, waiting for transfers between devices, shards(): totals = lax.psum(totals.astype(jnp.bfloat16), 'dp').astype(jnp.float32)  62.2 us
    concatenate x1, local copies, waits for them, and re-layouts, weight_terms(): jnp.concatenate([product(hidden_one, proj_cot), product(hidden_one, rate_...  48 us
  transfers between devices with their start and end apart: 8, of which 5 were waited for; matrix products, arithmetic and copies ran while one was open for 6% of the time, Pallas kernels for 0%

commit v1 on v0

--- a/solution.py
+++ b/solution.py
@@ -277,7 +277,10 @@
     first_section = lax.axis_index("section") == 0
     weights = (
         lax.all_gather(norm_gains[0], "fsdp", axis=1, tiled=True),
-        lax.all_gather(proj_weight[0], "fsdp", axis=0, tiled=True),
+        jnp.concatenate(
+            lax.all_to_all(jnp.stack([proj_weight[0]] * lax.axis_size("fsdp")), "fsdp", 0, 0),
+            axis=0,
+        ),
         lax.all_gather(rate_weight[0], "fsdp", axis=0, tiled=True),
         lax.all_gather(out_weight[0], "fsdp", axis=0, tiled=True),
         lax.all_gather(up_weight[0], "fsdp", axis=0, tiled=True),

time: 1470 us -> 1470 us (level)
  waiting for transfers between devices: 850 us -> 583 us
  blocking collectives: 106 us -> 366 us
    all_gather x1, waiting for transfers between devices: 173 us -> 0.02 us  [shards(): lax.all_gather(up_weight[0], 'fsdp', axis=0, tiled=True)]
    all_gather x1, blocking collectives: 12.7 us -> 177 us  [shards(): lax.all_gather(norm_gains[0], 'fsdp', axis=1, tiled=True)]
    all_gather x1, blocking collectives: 13.7 us -> 110 us  [shards(): lax.all_gather(rate_weight[0], 'fsdp', axis=0, tiled=True)]
    all_gather x1 -> x0, waiting for transfers between devices: 86.5 us -> none  [shards(): lax.all_gather(proj_weight[0], 'fsdp', axis=0, tiled=True)]
  transfers between devices with their start and end apart: 8 -> 8, of which waited for: 5 -> 3; matrix products, arithmetic and copies ran while one was open for 6% -> 6% of each run, Pallas kernels for 0% -> 0%
where the time goes in v1:
time: 1470 us; the launch traced here: 1460 us
  waiting for transfers between devices  583 us (40%)
  blocking collectives  366 us (25%)
  local copies, waits for them, and re-layouts  163 us (11%)
  matrix products  162 us (11%)
  other arithmetic  156 us (11%)
  between operations  17.3 us (1%)
    reduce_scatter x1, waiting for transfers between devices, shards(): lax.psum_scatter(term_of(jnp.int32(0), own_rows * lax.axis_size('fsdp'))....  427 us
    all_gather x1, blocking collectives, shards(): lax.all_gather(norm_gains[0], 'fsdp', axis=1, tiled=True)  177 us
    all_gather x1, blocking collectives, shards(): lax.all_gather(rate_weight[0], 'fsdp', axis=0, tiled=True)  110 us
    all_gather x1, waiting for transfers between devices, shards(): lax.all_gather(down_weight[0], 'fsdp', axis=0, tiled=True)  91.7 us
    another operation x6, other arithmetic, delta_rule(): lax.linalg.triangular_solve(system, right_side, left_side=True, lower=Tru...  83.2 us
    psum x1, blocking collectives, shards(): lax.psum((small_sum[0], small_sum[1], small_sum[2]), ('fsdp', 'dp'))  79.9 us
    psum x1, waiting for transfers between devices, shards(): totals = lax.psum(totals.astype(jnp.bfloat16), 'dp').astype(jnp.float32)  62.2 us
    concatenate x1, local copies, waits for them, and re-layouts, weight_terms(): jnp.concatenate([product(hidden_one, proj_cot), product(hidden_one, rate_...  47.9 us
  transfers between devices with their start and end apart: 8, of which 3 were waited for; matrix products, arithmetic and copies ran while one was open for 6% of the time, Pallas kernels for 0%

profile of v1, /device:TPU:0, one launch (start us, length us, event | category | flops | bytes accessed | tf_op | source)
XLA Modules:
  0.0 1460.6 jit_solution(11504457311469812191)
XLA Ops:
  12.1 6.5 all-to-all-start
  19.4 176.6 %all-gather = bf16[1,2,1024]{2,1,0:T(2,128)(2,1)S(1)} all-gather(bf16[1,2,256]{2,1,0:T(2,128)(2,1)S(1)} %copy-done.261), channel_id=2, replica_groups=mesh['section'=2,'fsdp'=4,'dp'=4] {'fsdp'}, dimensions={2}, use_global_device_ids=true | all-gather | bytes 5120 | tf_op jit(solution)/shard_map/all_gather | solution.py:279
  196.0 109.7 %all-gather.1 = bf16[1,1024,8]{1,2,0:T(8,128)(2,1)S(1)} all-gather(bf16[1,256,8]{1,2,0:T(8,128)(2,1)S(1)} %copy-done.254), channel_id=3, replica_groups=mesh['section'=2,'fsdp'=4,'dp'=4] {'fsdp'}, dimensions={1}, use_global_device_ids=true | all-gather | bytes 20480 | tf_op jit(solution)/shard_map/all_gather | solution.py:284
  323.4 39.3 %custom-call.16 = f32[1,4,2,1,64,64]{4,5,3,2,1,0:T(8,128)S(1)} custom-call(f32[1,4,2,1,64,64]{5,4,3,2,1,0:T(8,128)S(1)} %fusion.405), custom_call_target="InvertDiagBlocksLowerTriangular" | custom-call | tf_op jit(solution)/shard_map/jvp()/triangular_solve/custom-call.1 | solution.py:65
  367.2 7.0 while.96
  383.8 7.2 fusion.166
  393.1 91.7 %all-gather.13.cloned.1.call-done = bf16[1,1024,2816]{2,1,0:T(8,128)(2,1)} async-done(((bf16[1,256,2816]{2,1,0:T(8,128)(2,1)}), bf16[1,1024,2816]{2,1,0:T(8,128)(2,1)}) %all-gather.13.cloned.1.call-update) | async-done | bytes 5767184 | tf_op jit(solution)/shard_map/all_gather | solution.py:287
  484.8 4.6 fusion.228
  519.3 40.7 %custom-call.17 = f32[1,4,2,1,64,64]{4,5,3,2,1,0:T(8,128)} custom-call(f32[1,4,2,1,64,64]{5,4,3,2,1,0:T(8,128)} %fusion.393), custom_call_target="InvertDiagBlocksLowerTriangular" | custom-call | tf_op jit(solution)/shard_map/jvp()/triangular_solve/custom-call.1 | solution.py:65
  579.6 11.5 while.97
  603.4 6.1 fusion.169
  625.6 26.3 %while.98 = (s32[]{:T(128)}, f32[1,4,128,256]{2,3,1,0:T(8,128)S(1)}, f32[2,1,4,64,128]{4,3,0,2,1:T(8,128)}, f32[2,1,4,64,128]{4,3,2,1,0:T(8,128)}, f32[2,1,4,64,...) while((s32[]{:T(128)}, ...), condition=%wide.region_20.23_spmd.clone, body=%wide.region_18.22_spmd.clone.sunk | while | flops 706019328 | bytes 25702096 | solution.py:93
  687.0 6.1 fusion.279
  707.0 4.9 fusion.436
  725.3 19.1 %while.99 = (s32[]{:T(128)}, f32[1,4,128,256]{2,3,1,0:T(8,128)S(1)}, f32[2,1,4,64,128]{4,3,0,2,1:T(8,128)}, f32[2,1,4,64,128]{4,3,2,1,0:T(8,128)}, f32[2,1,4,64,...) while((s32[]{:T(128)}, ...), condition=%wide.region_37.42_spmd.clone, body=%wide.region_35.41_spmd.clone.sunk | while | flops 706019328 | bytes 25701472 | solution.py:93
  766.8 5.2 multiply_reduce_fusion.3
  773.8 5.8 fusion.277
  802.0 6.9 convolution_convert_fusion
  809.1 5.9 convolution_convert_fusion.1
  815.0 47.9 %concatenate.48 = bf16[1024,12554]{1,0:T(8,128)(2,1)} concatenate(bf16[1024,3072]{1,0:T(8,128)(2,1)} %convolution_convert_fusion.2, bf16[1024,8]{1,0:T(8,128)(2,1)S(1)} %copy.593, bf16[1024,1024]{1,0:T(8,128)(2,1)S(1)} %copy-done.41, bf16[1024,5632]{1,0:T(8,128)(2,1)} %convolution_convert_fusion, bf16[1024,2816]{1,0:T(8,128)(2,1)} %convolution_convert_fusion.1, ...), dimensions={1} | concatenate | bytes 51421184 | tf_op jit(solution)/shard_map/concatenate | solution.py:233
  863.0 427.1 %reduce-scatter.2.cloned.1.call-done = bf16[256,12554]{1,0:T(8,128)(2,1)} async-done(((bf16[1024,12554]{1,0:T(8,128)(2,1)}), bf16[256,12554]{1,0:T(8,128)(2,1)}) %reduce-scatter.2.cloned.1.call-update) | async-done | bytes 6427664 | tf_op jit(solution)/shard_map/reduce_scatter | solution.py:334
  1291.4 5.3 fusion.250
  1296.9 79.9 %all-reduce.51 = (f32[1,4,2048]{2,1,0:T(4,128)}, f32[1,2,4]{2,1,0:T(2,128)}, f32[1,256]{1,0:T(1,128)}) all-reduce(f32[1,4,2048]{2,1,0:T(4,128)S(1)} %add_bitcast_fusion.2, f32[1,2,4]{2,1,0:T(2,128)S(1)} %add_bitcast_fusion.3, f32[1,256]{1,0:T(1,128)S(1)} %bitcast.1636), channel_id=1, replica_groups=mesh['section'=2,'fsdp'=4,'dp'=4] {'fsdp','dp'}, use_global_device_ids=true, to_apply=%region_64.69 | all-reduce | flops 8456 | bytes 67648 | tf_op jit(solution)/shard_map/psum | solution.py:341
  1376.8 62.2 %all-reduce.54.cloned.1.call-done = bf16[256,12554]{1,0:T(8,128)(2,1)} async-done(((bf16[256,12554]{1,0:T(8,128)(2,1)}), bf16[256,12554]{1,0:T(8,128)(2,1)}) %all-reduce.54.cloned.1.call-update) | async-done | bytes 6427664 | tf_op jit(solution)/shard_map/psum | solution.py:340
  (1028 shorter events, 301.0 us)
Async XLA Ops:
  7.2 373.9 %all-gather.9.cloned.1.call-start = ((), (), s32[]{:S(2)}) async-start(), calls=%async_computation.4 | async-start | bytes 2621440 | tf_op jit(solution)/shard_map/all_gather | solution.py:285
  7.9 375.9 %all-gather.11.cloned.1.call-start = ((), (), s32[]{:S(2)}) async-start(), calls=%async_computation.5 | async-start | bytes 14417920 | tf_op jit(solution)/shard_map/all_gather | solution.py:286
  12.1 183.9 %copy-start.254 = (bf16[1,256,8]{1,2,0:T(8,128)(2,1)S(1)}, bf16[1,256,8]{1,2,0:T(8,128)(2,1)}, u32[]{:S(2)}) copy-start(bf16[1,256,8]{1,2,0:T(8,128)(2,1)} %param.32) | copy-start | bytes 12292
  12.1 293.6 %copy-start.18 = (bf16[1,1,128,1024]{3,2,1,0:T(8,128)(2,1)S(1)}, bf16[1,1,128,1024]{3,2,1,0:T(8,128)(2,1)}, u32[]{:S(2)}) copy-start(bf16[1,1,128,1024]{3,2,1,0:T(8,128)(2,1)} %param.27) | copy-start | bytes 786436
  12.1 298.6 %all-to-all-start = ((bf16[4,256,3072]{2,1,0:T(8,128)(2,1)}), bf16[4,256,3072]{2,1,0:T(8,128)(2,1)}, u32[]{:S(2)}, u32[]{:S(2)}) async-start(bf16[4,256,3072]{2,1,0:T(8,128)(2,1)} %stack.21), calls=%async_computation | async-start | bytes 12582912 | tf_op jit(solution)/shard_map/all_to_all | solution.py:281
  18.6 288.2 %copy-start.255 = (f32[1,2,4]{2,1,0:T(2,128)S(1)}, f32[1,2,4]{2,1,0:T(2,128)}, u32[]{:S(2)}) copy-start(f32[1,2,4]{2,1,0:T(2,128)} %param.37) | copy-start | bytes 100
  18.6 288.2 %copy-start.260 = (s32[1,1,128]{2,1,0:T(1,128)S(1)}, s32[1,1,128]{2,1,0:T(1,128)}, u32[]{:S(2)}) copy-start(s32[1,1,128]{2,1,0:T(1,128)} %param.28) | copy-start | bytes 1540
  18.6 292.0 %copy-start.188 = (f32[1,4,2048]{2,1,0:T(4,128)S(1)}, f32[1,4,2048]{2,1,0:T(4,128)}, u32[]{:S(2)}) copy-start(f32[1,4,2048]{2,1,0:T(4,128)} %param.36) | copy-start | bytes 98308
  18.6 466.2 %all-gather.13.cloned.1.call-start = ((), (), s32[]{:S(2)}) async-start(), calls=%async_computation.6 | async-start | bytes 7208960 | tf_op jit(solution)/shard_map/all_gather | solution.py:287
  19.3 1270.8 %reduce-scatter.2.cloned.1.call-start = ((), (), s32[]{:S(2)}) async-start(), calls=%async_computation.2 | async-start | bytes 32440320 | tf_op jit(solution)/shard_map/reduce_scatter | solution.py:334
  305.7 189.9 %copy-start.154 = (bf16[1,1024,8]{1,2,0:T(8,128)(2,1)}, bf16[1,1024,8]{1,2,0:T(8,128)(2,1)S(1)}, u32[]{:S(2)}) copy-start(bf16[1,1024,8]{1,2,0:T(8,128)(2,1)S(1)} %all-gather.1) | copy-start | bytes 49156
  306.5 77.3 %copy-start.146 = (f32[1,1,1024]{2,1,0:T(1,128)}, f32[1,1,1024]{2,1,0:T(1,128)S(1)}, u32[]{:S(2)}) copy-start(f32[1,1,1024]{2,1,0:T(1,128)S(1)} %get-tuple-element.1629) | copy-start | bytes 12292
  306.5 189.0 %copy-start.144 = (f32[1,1,1024]{2,1,0:T(1,128)}, f32[1,1,1024]{2,1,0:T(1,128)S(1)}, u32[]{:S(2)}) copy-start(f32[1,1,1024]{2,1,0:T(1,128)S(1)} %get-tuple-element.1630) | copy-start | bytes 12292
  309.5 53.3 %copy-start.150 = (f32[4,2,64]{2,1,0:T(2,128)}, f32[4,2,64]{2,1,0:T(2,128)S(1)}, u32[]{:S(2)}) copy-start(f32[4,2,64]{2,1,0:T(2,128)S(1)} %mul.1580) | copy-start | bytes 6148
  320.0 44.0 %copy-start.58 = (f32[1,4,128,128]{3,1,2,0:T(4,128)}, f32[1,4,128,128]{3,1,2,0:T(4,128)S(1)}, u32[]{:S(2)}) copy-start(f32[1,4,128,128]{3,1,2,0:T(4,128)S(1)} %get-tuple-element.1663) | copy-start | bytes 786436
  321.3 42.5 %copy-start.78 = (f32[1,128,4,256]{3,2,1,0:T(4,128)}, f32[1,128,4,256]{3,2,1,0:T(4,128)S(1)}, u32[]{:S(2)}) copy-start(f32[1,128,4,256]{3,2,1,0:T(4,128)S(1)} %reshape.2344) | copy-start | bytes 1572868
  383.7 101.0 %copy-start.2 = (f32[128,1024]{1,0:T(8,128)}, f32[128,1024]{1,0:T(8,128)S(1)}, u32[]{:S(2)}) copy-start(f32[128,1024]{1,0:T(8,128)S(1)} %get-tuple-element.1649) | copy-start | bytes 1572868
  393.0 96.3 %copy-start.67 = (bf16[1,128,2816]{2,1,0:T(8,128)(2,1)}, bf16[1,128,2816]{2,1,0:T(8,128)(2,1)S(1)}, u32[]{:S(2)}) copy-start(bf16[1,128,2816]{2,1,0:T(8,128)(2,1)S(1)} %multiply_convert_fusion.1) | copy-start | bytes 2162692
  489.4 5.9 collective-permute-start
  510.3 64.0 %copy-start = (f32[1,4,128,128]{3,1,2,0:T(4,128)}, f32[1,4,128,128]{3,1,2,0:T(4,128)S(1)}, u32[]{:S(2)}) copy-start(f32[1,4,128,128]{3,1,2,0:T(4,128)S(1)} %bitcast_multiply_fusion.30) | copy-start | bytes 786436
  512.1 49.6 %copy-start.54 = (f32[1,4,128,128]{3,1,2,0:T(4,128)}, f32[1,4,128,128]{3,1,2,0:T(4,128)S(1)}, u32[]{:S(2)}) copy-start(f32[1,4,128,128]{3,1,2,0:T(4,128)S(1)} %fusion.387) | copy-start | bytes 786436
  517.6 44.2 %copy-start.110 = (f32[4,2,64,64]{3,2,1,0:T(8,128)}, f32[4,2,64,64]{3,2,1,0:T(8,128)S(1)}, u32[]{:S(2)}) copy-start(f32[4,2,64,64]{3,2,1,0:T(8,128)S(1)} %fusion.350) | copy-start | bytes 393220
  702.3 4.6 collective-permute-start.1
  863.0 576.0 %all-reduce.54.cloned.1.call-start = ((), (), s32[]{:S(2)}) async-start(), calls=%async_computation.3 | async-start | bytes 12976128 | tf_op jit(solution)/shard_map/psum | solution.py:340
  (308 other events, 1356.2 us)
Sparse Core Ops, SparseCore 0:
  9.6 98.5 all-gather.8
  109.7 267.5 all-gather.10
  378.9 105.8 all-gather.12
  863.1 426.9 reduce-scatter.1
  1293.3 145.6 all-reduce.53
